TPU v7x, 256 devices: a whole 4x4x8 slice. The times are simulated.
256 devices in a mesh: tile: 64 (over y, z, core), sec: 4 (over x).
Axes of the slice: x: 4, y: 4, z: 8, core: 2. Of those that a mesh axis runs over, the one named last changes fastest.
Arguments:
- voltage: float32 [8192, 512], P('tile', 'sec'), may hold values from -6 to 6
- conductance: float32 [8192, 512], P('tile', 'sec'), may hold values from 0.2 to 2
- reversal: float32 [8192, 512], P('tile', 'sec'), may hold values from -1 to 1
- drive: bfloat16 [8, 8192, 512], P(None, 'tile', 'sec'), may hold values from -6 to 6
- inv_cable: float32 [128, 128], replicated, may hold values from -1 to 1
- owner_map: int32 [8192], P('tile'), may hold values from 0 to 63, as said below
- peer_counts: int32 [64, 64], P('tile'), may hold values from 0 to 4, as said below
- pattern: int32 [4, 8192, 2], P('sec', 'tile'), may hold values from 0 to 31, all different within a row
- transfer: bfloat16 [4, 8192, 2, 128, 128], P('sec', 'tile'), may hold values from -0.01171875 to 0.01171875
Outputs:
- final_voltage: float32 [8192, 512], P('tile', 'sec')
- probe: float32 [8, 4096], P(None, ('tile', 'sec'))
Inputs may be any that keep to these rules, and one draw needn't show every extreme that they name: `owner_map`: every depth tile owns exactly 128 cells; the cells c with c // 128 = u include at most 4 cells of one owner, and exactly 4 of some owner. peer_counts[d, u] is the number of cells c with c // 128 = u and owner_map[c] = d. `pattern`: the 2 contact tiles of one slot and section differ.
All inputs are finite; a program needn't handle non-finite values.
Results may differ from a plain program's by a relative error of at most 0.0029.
Values may be sent and summed in bfloat16 or wider, within the bound.
A program may use at most 64 MiB of HBM per device.

v0:
```python
import jax
import jax.numpy as jnp
from jax import lax
from jax.sharding import PartitionSpec as P

CONTACTS = 4096
TIME_STEP = 0.25
AXIAL = 2.0


def padded_2(block, sides, width):
    for axis, dim in sides:
        count = lax.axis_size(axis)
        forward = [(i, i + 1) for i in range(count - 1)]
        backward = [(target, source) for source, target in forward]
        low = lax.ppermute(
            lax.slice_in_dim(block, block.shape[dim] - width, None, axis=dim), axis, forward
        )
        high = lax.ppermute(lax.slice_in_dim(block, 0, width, axis=dim), axis, backward)
        block = jnp.concatenate([low, block, high], axis=dim)
    return block


def cable_update(voltage_now, conductance, reversal, drive_now, inv_cable):
    padded = padded_2(voltage_now.astype(jnp.bfloat16), (("sec", 1),), 1).astype(voltage_now.dtype)
    columns = jnp.arange(voltage_now.shape[1], dtype=jnp.int32)
    first_col = (columns == 0).astype(jnp.float32)
    last_col = (columns == voltage_now.shape[1] - 1).astype(jnp.float32)
    boundary = first_col * (padded[:, :-2] - voltage_now) + last_col * (padded[:, 2:] - voltage_now)
    driven = drive_now.astype(jnp.float32)
    right_side = voltage_now * (1.0 - TIME_STEP * conductance) + TIME_STEP * (
        conductance * reversal + driven + AXIAL * boundary
    )
    voltage_next = jnp.einsum("ci,ji->cj", right_side, inv_cable, precision=lax.Precision.HIGHEST)
    current = (conductance * (voltage_next - reversal) - driven).astype(jnp.bfloat16)
    return (voltage_next, current)


def on_device(
    voltage, conductance, reversal, drive, inv_cable, owner_map, peer_counts, pattern, transfer
):
    cell_count = voltage.shape[0]
    seg_width = voltage.shape[1]
    step_count = drive.shape[0]
    tile_count = lax.axis_size("tile")
    section_count = lax.axis_size("sec")
    capacity = 2 * cell_count // tile_count
    owners = jnp.arange(tile_count, dtype=jnp.int32)
    member = (owner_map[:, None] == owners[None, :]).astype(jnp.int32)
    rank_within = jnp.sum(jnp.cumsum(member, axis=0) * member, axis=1) - 1
    placed = owner_map * capacity + rank_within
    source_row = (
        jnp.full((tile_count * capacity,), cell_count, jnp.int32)
        .at[placed]
        .set(jnp.arange(cell_count, dtype=jnp.int32))
    )
    blank_row = jnp.zeros((1, seg_width), jnp.bfloat16)

    def advance_send(voltage_now, drive_now):
        voltage_next, current = cable_update(
            voltage_now, conductance, reversal, drive_now, inv_cable
        )
        outgoing = jnp.take(jnp.concatenate([current, blank_row], axis=0), source_row, axis=0)
        outgoing = outgoing.reshape(tile_count, capacity, seg_width)
        arrived = lax.all_to_all(outgoing, "tile", split_axis=0, concat_axis=0, tiled=True)
        return (voltage_next, arrived)

    final_voltage, arrived = lax.scan(advance_send, voltage, drive)
    received = arrived.reshape(step_count, tile_count * capacity, seg_width)
    counts = peer_counts[0]
    end_rows = jnp.cumsum(counts)
    starts = end_rows - counts
    slot_ids = jnp.arange(cell_count, dtype=jnp.int32)
    source = jnp.sum((end_rows[None, :] <= slot_ids[:, None]).astype(jnp.int32), axis=1)
    offset = jnp.sum(jnp.where(source[:, None] == owners[None, :], starts[None, :], 0), axis=1)
    gather_rows = source * capacity + slot_ids - offset
    ordered = jnp.take(received, gather_rows, axis=1)
    weights = transfer[0]
    layout = pattern[0]
    contact_width = weights.shape[3]
    tile_total = CONTACTS // contact_width
    tile_sums = jnp.einsum("tsi,skic->tskc", ordered, weights, preferred_element_type=jnp.float32)
    select = (layout[:, :, None] == jnp.arange(tile_total, dtype=jnp.int32)[None, None, :]).astype(
        jnp.float32
    )
    partial_sum = jnp.einsum("tskc,skq->tqc", tile_sums, select, precision=lax.Precision.HIGHEST)
    partial_sum = partial_sum.reshape(step_count, tile_total * contact_width)
    summed = lax.psum(partial_sum, ("tile", "sec"))
    share_width = summed.shape[1] // (tile_count * section_count)
    position = lax.axis_index("tile") * section_count + lax.axis_index("sec")
    probe_share = lax.dynamic_slice_in_dim(summed, position * share_width, share_width, 1)
    return (final_voltage, probe_share)


def solution(mesh):
    placed = (
        P("tile", "sec"),
        P("tile", "sec"),
        P("tile", "sec"),
        P(None, "tile", "sec"),
        P(),
        P("tile"),
        P("tile", None),
        P("sec", "tile", None),
        P("sec", "tile", None, None, None),
    )
    return jax.shard_map(
        on_device,
        mesh=mesh,
        in_specs=placed,
        out_specs=(P("tile", "sec"), P(None, ("tile", "sec"))),
        check_vma=False,
    )
```

profile of v0, /device:TPU:8, one launch (start us, length us, event | category | flops | bytes accessed | tf_op | source)
XLA Modules:
  0.0 478.0 jit_solution(9085325909894427495)
XLA Ops:
  7.2 0.8 copy.37
  10.9 0.8 select_reduce_fusion.1
  12.4 0.9 mul.74
  13.3 1.0 scatter_custom_fusion
  14.3 208.3 %while.13 = (s32[]{:T(128)}, f32[128,128]{1,0:T(8,128)S(1)}, bf16[8,64,4,128]{3,2,1,0:T(4,128)(2,1)S(1)}, f32[128,128]{1,0:T(8,128)}, bf16[8,128,128]{2,1,0:T(8,...) while((s32[]{:T(128)}, f32[128,128]{1,0:T(8,128)S(1)}, ...), condition=%wide.region_4.5_spmd, body=%wide.region_3.4_spmd.sunk | while | flops 25629952 | bytes 1626603 | solution.py:68
  14.4 1.3 collective-permute-start
  15.7 4.5 collective-permute-start.1
  20.4 1.4 collective-permute-done.1
  21.9 1.3 fusion.52
  23.2 0.9 gather_fusion
  24.8 12.1 %all-to-all-start = ((bf16[64,4,128]{2,1,0:T(4,128)(2,1)}), bf16[64,4,128]{2,1,0:T(4,128)(2,1)S(1)}, u32[]{:S(2)}, u32[]{:S(2)}) async-start(bf16[64,4,128]{2,1,0:T(4,128)(2,1)} %broadcast_select_fusion.2), calls=%async_computation | async-start | bytes 131072 | tf_op jit(solution)/shard_map/while/body/eval_jaxpr/all_to_all | solution.py:65
  36.9 8.8 %all-to-all-done = bf16[64,4,128]{2,1,0:T(4,128)(2,1)S(1)} async-done(((bf16[64,4,128]{2,1,0:T(4,128)(2,1)}), bf16[64,4,128]{2,1,0:T(4,128)(2,1)S(1)}, u32[]{:S(2)}, u32[]{:S(2)}) %all-to-all-start) | async-done | bytes 65568 | tf_op jit(solution)/shard_map/while/body/eval_jaxpr/all_to_all | solution.py:65
  45.9 1.3 collective-permute-start
  47.2 4.9 %collective-permute-start.1 = (bf16[128,1]{1,0:T(8,128)(2,1)S(1)}, bf16[128,1]{1,0:T(8,128)(2,1)S(1)}, u32[]{:S(2)}, u32[]{:S(2)}) collective-permute-start(bf16[128,1]{1,0:T(8,128)(2,1)S(1)} %get-tuple-element.171), channel_id=1, source_target_pairs={{0,1},{1,2},{2,3},{4,5},{5,6},{6,7},{8,9},{9,10},{10,11},{12,13},{... | collective-permute-start | bytes 776 | tf_op jit(solution)/shard_map/while/body/eval_jaxpr/ppermute | solution.py:16
  52.2 1.4 collective-permute-done.1
  53.7 1.3 fusion.52
  55.0 0.9 gather_fusion
  56.7 5.5 %all-to-all-start = ((bf16[64,4,128]{2,1,0:T(4,128)(2,1)}), bf16[64,4,128]{2,1,0:T(4,128)(2,1)S(1)}, u32[]{:S(2)}, u32[]{:S(2)}) async-start(bf16[64,4,128]{2,1,0:T(4,128)(2,1)} %broadcast_select_fusion.2), calls=%async_computation | async-start | bytes 131072 | tf_op jit(solution)/shard_map/while/body/eval_jaxpr/all_to_all | solution.py:65
  62.2 8.8 %all-to-all-done = bf16[64,4,128]{2,1,0:T(4,128)(2,1)S(1)} async-done(((bf16[64,4,128]{2,1,0:T(4,128)(2,1)}), bf16[64,4,128]{2,1,0:T(4,128)(2,1)S(1)}, u32[]{:S(2)}, u32[]{:S(2)}) %all-to-all-start) | async-done | bytes 65568 | tf_op jit(solution)/shard_map/while/body/eval_jaxpr/all_to_all | solution.py:65
  71.2 1.3 collective-permute-start
  72.5 4.9 %collective-permute-start.1 = (bf16[128,1]{1,0:T(8,128)(2,1)S(1)}, bf16[128,1]{1,0:T(8,128)(2,1)S(1)}, u32[]{:S(2)}, u32[]{:S(2)}) collective-permute-start(bf16[128,1]{1,0:T(8,128)(2,1)S(1)} %get-tuple-element.171), channel_id=1, source_target_pairs={{0,1},{1,2},{2,3},{4,5},{5,6},{6,7},{8,9},{9,10},{10,11},{12,13},{... | collective-permute-start | bytes 776 | tf_op jit(solution)/shard_map/while/body/eval_jaxpr/ppermute | solution.py:16
  77.5 1.4 collective-permute-done.1
  79.0 1.3 fusion.52
  80.3 0.9 gather_fusion
  81.9 5.5 %all-to-all-start = ((bf16[64,4,128]{2,1,0:T(4,128)(2,1)}), bf16[64,4,128]{2,1,0:T(4,128)(2,1)S(1)}, u32[]{:S(2)}, u32[]{:S(2)}) async-start(bf16[64,4,128]{2,1,0:T(4,128)(2,1)} %broadcast_select_fusion.2), calls=%async_computation | async-start | bytes 131072 | tf_op jit(solution)/shard_map/while/body/eval_jaxpr/all_to_all | solution.py:65
  87.4 8.8 %all-to-all-done = bf16[64,4,128]{2,1,0:T(4,128)(2,1)S(1)} async-done(((bf16[64,4,128]{2,1,0:T(4,128)(2,1)}), bf16[64,4,128]{2,1,0:T(4,128)(2,1)S(1)}, u32[]{:S(2)}, u32[]{:S(2)}) %all-to-all-start) | async-done | bytes 65568 | tf_op jit(solution)/shard_map/while/body/eval_jaxpr/all_to_all | solution.py:65
  96.4 1.3 collective-permute-start
  97.7 4.9 %collective-permute-start.1 = (bf16[128,1]{1,0:T(8,128)(2,1)S(1)}, bf16[128,1]{1,0:T(8,128)(2,1)S(1)}, u32[]{:S(2)}, u32[]{:S(2)}) collective-permute-start(bf16[128,1]{1,0:T(8,128)(2,1)S(1)} %get-tuple-element.171), channel_id=1, source_target_pairs={{0,1},{1,2},{2,3},{4,5},{5,6},{6,7},{8,9},{9,10},{10,11},{12,13},{... | collective-permute-start | bytes 776 | tf_op jit(solution)/shard_map/while/body/eval_jaxpr/ppermute | solution.py:16
  102.8 1.4 collective-permute-done.1
  104.3 1.3 fusion.52
  105.5 0.9 gather_fusion
  107.2 5.5 %all-to-all-start = ((bf16[64,4,128]{2,1,0:T(4,128)(2,1)}), bf16[64,4,128]{2,1,0:T(4,128)(2,1)S(1)}, u32[]{:S(2)}, u32[]{:S(2)}) async-start(bf16[64,4,128]{2,1,0:T(4,128)(2,1)} %broadcast_select_fusion.2), calls=%async_computation | async-start | bytes 131072 | tf_op jit(solution)/shard_map/while/body/eval_jaxpr/all_to_all | solution.py:65
  112.7 8.8 %all-to-all-done = bf16[64,4,128]{2,1,0:T(4,128)(2,1)S(1)} async-done(((bf16[64,4,128]{2,1,0:T(4,128)(2,1)}), bf16[64,4,128]{2,1,0:T(4,128)(2,1)S(1)}, u32[]{:S(2)}, u32[]{:S(2)}) %all-to-all-start) | async-done | bytes 65568 | tf_op jit(solution)/shard_map/while/body/eval_jaxpr/all_to_all | solution.py:65
  121.7 1.3 collective-permute-start
  123.0 4.9 %collective-permute-start.1 = (bf16[128,1]{1,0:T(8,128)(2,1)S(1)}, bf16[128,1]{1,0:T(8,128)(2,1)S(1)}, u32[]{:S(2)}, u32[]{:S(2)}) collective-permute-start(bf16[128,1]{1,0:T(8,128)(2,1)S(1)} %get-tuple-element.171), channel_id=1, source_target_pairs={{0,1},{1,2},{2,3},{4,5},{5,6},{6,7},{8,9},{9,10},{10,11},{12,13},{... | collective-permute-start | bytes 776 | tf_op jit(solution)/shard_map/while/body/eval_jaxpr/ppermute | solution.py:16
  128.0 1.4 collective-permute-done.1
  129.5 1.3 fusion.52
  130.8 0.9 gather_fusion
  132.4 5.5 %all-to-all-start = ((bf16[64,4,128]{2,1,0:T(4,128)(2,1)}), bf16[64,4,128]{2,1,0:T(4,128)(2,1)S(1)}, u32[]{:S(2)}, u32[]{:S(2)}) async-start(bf16[64,4,128]{2,1,0:T(4,128)(2,1)} %broadcast_select_fusion.2), calls=%async_computation | async-start | bytes 131072 | tf_op jit(solution)/shard_map/while/body/eval_jaxpr/all_to_all | solution.py:65
  137.9 8.8 %all-to-all-done = bf16[64,4,128]{2,1,0:T(4,128)(2,1)S(1)} async-done(((bf16[64,4,128]{2,1,0:T(4,128)(2,1)}), bf16[64,4,128]{2,1,0:T(4,128)(2,1)S(1)}, u32[]{:S(2)}, u32[]{:S(2)}) %all-to-all-start) | async-done | bytes 65568 | tf_op jit(solution)/shard_map/while/body/eval_jaxpr/all_to_all | solution.py:65
  146.9 1.3 collective-permute-start
  148.2 4.9 %collective-permute-start.1 = (bf16[128,1]{1,0:T(8,128)(2,1)S(1)}, bf16[128,1]{1,0:T(8,128)(2,1)S(1)}, u32[]{:S(2)}, u32[]{:S(2)}) collective-permute-start(bf16[128,1]{1,0:T(8,128)(2,1)S(1)} %get-tuple-element.171), channel_id=1, source_target_pairs={{0,1},{1,2},{2,3},{4,5},{5,6},{6,7},{8,9},{9,10},{10,11},{12,13},{... | collective-permute-start | bytes 776 | tf_op jit(solution)/shard_map/while/body/eval_jaxpr/ppermute | solution.py:16
  153.3 1.4 collective-permute-done.1
  154.8 1.3 fusion.52
  156.1 0.9 gather_fusion
  157.7 5.5 %all-to-all-start = ((bf16[64,4,128]{2,1,0:T(4,128)(2,1)}), bf16[64,4,128]{2,1,0:T(4,128)(2,1)S(1)}, u32[]{:S(2)}, u32[]{:S(2)}) async-start(bf16[64,4,128]{2,1,0:T(4,128)(2,1)} %broadcast_select_fusion.2), calls=%async_computation | async-start | bytes 131072 | tf_op jit(solution)/shard_map/while/body/eval_jaxpr/all_to_all | solution.py:65
  163.2 8.8 %all-to-all-done = bf16[64,4,128]{2,1,0:T(4,128)(2,1)S(1)} async-done(((bf16[64,4,128]{2,1,0:T(4,128)(2,1)}), bf16[64,4,128]{2,1,0:T(4,128)(2,1)S(1)}, u32[]{:S(2)}, u32[]{:S(2)}) %all-to-all-start) | async-done | bytes 65568 | tf_op jit(solution)/shard_map/while/body/eval_jaxpr/all_to_all | solution.py:65
  172.2 1.3 collective-permute-start
  173.5 4.9 %collective-permute-start.1 = (bf16[128,1]{1,0:T(8,128)(2,1)S(1)}, bf16[128,1]{1,0:T(8,128)(2,1)S(1)}, u32[]{:S(2)}, u32[]{:S(2)}) collective-permute-start(bf16[128,1]{1,0:T(8,128)(2,1)S(1)} %get-tuple-element.171), channel_id=1, source_target_pairs={{0,1},{1,2},{2,3},{4,5},{5,6},{6,7},{8,9},{9,10},{10,11},{12,13},{... | collective-permute-start | bytes 776 | tf_op jit(solution)/shard_map/while/body/eval_jaxpr/ppermute | solution.py:16
  178.5 1.4 collective-permute-done.1
  180.0 1.3 fusion.52
  181.3 0.9 gather_fusion
  182.9 5.5 %all-to-all-start = ((bf16[64,4,128]{2,1,0:T(4,128)(2,1)}), bf16[64,4,128]{2,1,0:T(4,128)(2,1)S(1)}, u32[]{:S(2)}, u32[]{:S(2)}) async-start(bf16[64,4,128]{2,1,0:T(4,128)(2,1)} %broadcast_select_fusion.2), calls=%async_computation | async-start | bytes 131072 | tf_op jit(solution)/shard_map/while/body/eval_jaxpr/all_to_all | solution.py:65
  188.5 8.8 %all-to-all-done = bf16[64,4,128]{2,1,0:T(4,128)(2,1)S(1)} async-done(((bf16[64,4,128]{2,1,0:T(4,128)(2,1)}), bf16[64,4,128]{2,1,0:T(4,128)(2,1)S(1)}, u32[]{:S(2)}, u32[]{:S(2)}) %all-to-all-start) | async-done | bytes 65568 | tf_op jit(solution)/shard_map/while/body/eval_jaxpr/all_to_all | solution.py:65
  197.5 1.3 collective-permute-start
  198.7 4.9 %collective-permute-start.1 = (bf16[128,1]{1,0:T(8,128)(2,1)S(1)}, bf16[128,1]{1,0:T(8,128)(2,1)S(1)}, u32[]{:S(2)}, u32[]{:S(2)}) collective-permute-start(bf16[128,1]{1,0:T(8,128)(2,1)S(1)} %get-tuple-element.171), channel_id=1, source_target_pairs={{0,1},{1,2},{2,3},{4,5},{5,6},{6,7},{8,9},{9,10},{10,11},{12,13},{... | collective-permute-start | bytes 776 | tf_op jit(solution)/shard_map/while/body/eval_jaxpr/ppermute | solution.py:16
  203.8 1.4 collective-permute-done.1
  205.3 1.3 fusion.52
  206.6 0.9 gather_fusion
  208.2 5.5 %all-to-all-start = ((bf16[64,4,128]{2,1,0:T(4,128)(2,1)}), bf16[64,4,128]{2,1,0:T(4,128)(2,1)S(1)}, u32[]{:S(2)}, u32[]{:S(2)}) async-start(bf16[64,4,128]{2,1,0:T(4,128)(2,1)} %broadcast_select_fusion.2), calls=%async_computation | async-start | bytes 131072 | tf_op jit(solution)/shard_map/while/body/eval_jaxpr/all_to_all | solution.py:65
  213.7 8.8 %all-to-all-done = bf16[64,4,128]{2,1,0:T(4,128)(2,1)S(1)} async-done(((bf16[64,4,128]{2,1,0:T(4,128)(2,1)}), bf16[64,4,128]{2,1,0:T(4,128)(2,1)S(1)}, u32[]{:S(2)}, u32[]{:S(2)}) %all-to-all-start) | async-done | bytes 65568 | tf_op jit(solution)/shard_map/while/body/eval_jaxpr/all_to_all | solution.py:65
  223.9 4.6 fusion.28
  230.1 239.7 %all-reduce.3.cloned.1.call-done = f32[8,4096]{1,0:T(8,128)} async-done(((f32[8,4096]{1,0:T(8,128)}), f32[8,4096]{1,0:T(8,128)}) %all-reduce.3.cloned.1.call-update) | async-done | bytes 131088 | tf_op jit(solution)/shard_map/psum | solution.py:88
  469.8 1.3 constant_dynamic-slice_fusion
  (128 shorter events, 15.4 us)
Async XLA Ops:
  7.2 462.6 %all-reduce.3.cloned.1.call-start = ((), (), s32[]{:S(2)}) async-start(), calls=%async_computation.1 | async-start | bytes 262144 | tf_op jit(solution)/shard_map/psum | solution.py:88
  14.4 6.0 %collective-permute-start = (bf16[128,1]{1,0:T(8,128)(2,1)S(1)}, bf16[128,1]{1,0:T(8,128)(2,1)S(1)}, u32[]{:S(2)}, u32[]{:S(2)}) collective-permute-start(bf16[128,1]{1,0:T(8,128)(2,1)S(1)} %get-tuple-element.170), channel_id=1, source_target_pairs={{1,0},{2,1},{3,2},{5,4},{6,5},{7,6},{9,8},{10,9},{11,10},{13,12},{... | collective-permute-start | bytes 776 | tf_op jit(solution)/shard_map/while/body/eval_jaxpr/ppermute | solution.py:19
  15.7 6.1 %collective-permute-start.1 = (bf16[128,1]{1,0:T(8,128)(2,1)S(1)}, bf16[128,1]{1,0:T(8,128)(2,1)S(1)}, u32[]{:S(2)}, u32[]{:S(2)}) collective-permute-start(bf16[128,1]{1,0:T(8,128)(2,1)S(1)} %get-tuple-element.171), channel_id=1, source_target_pairs={{0,1},{1,2},{2,3},{4,5},{5,6},{6,7},{8,9},{9,10},{10,11},{12,13},{... | collective-permute-start | bytes 776 | tf_op jit(solution)/shard_map/while/body/eval_jaxpr/ppermute | solution.py:16
  24.8 20.9 %all-to-all-start = ((bf16[64,4,128]{2,1,0:T(4,128)(2,1)}), bf16[64,4,128]{2,1,0:T(4,128)(2,1)S(1)}, u32[]{:S(2)}, u32[]{:S(2)}) async-start(bf16[64,4,128]{2,1,0:T(4,128)(2,1)} %broadcast_select_fusion.2), calls=%async_computation | async-start | bytes 131072 | tf_op jit(solution)/shard_map/while/body/eval_jaxpr/all_to_all | solution.py:65
  45.9 6.3 %collective-permute-start = (bf16[128,1]{1,0:T(8,128)(2,1)S(1)}, bf16[128,1]{1,0:T(8,128)(2,1)S(1)}, u32[]{:S(2)}, u32[]{:S(2)}) collective-permute-start(bf16[128,1]{1,0:T(8,128)(2,1)S(1)} %get-tuple-element.170), channel_id=1, source_target_pairs={{1,0},{2,1},{3,2},{5,4},{6,5},{7,6},{9,8},{10,9},{11,10},{13,12},{... | collective-permute-start | bytes 776 | tf_op jit(solution)/shard_map/while/body/eval_jaxpr/ppermute | solution.py:19
  47.2 6.4 %collective-permute-start.1 = (bf16[128,1]{1,0:T(8,128)(2,1)S(1)}, bf16[128,1]{1,0:T(8,128)(2,1)S(1)}, u32[]{:S(2)}, u32[]{:S(2)}) collective-permute-start(bf16[128,1]{1,0:T(8,128)(2,1)S(1)} %get-tuple-element.171), channel_id=1, source_target_pairs={{0,1},{1,2},{2,3},{4,5},{5,6},{6,7},{8,9},{9,10},{10,11},{12,13},{... | collective-permute-start | bytes 776 | tf_op jit(solution)/shard_map/while/body/eval_jaxpr/ppermute | solution.py:16
  56.7 14.4 %all-to-all-start = ((bf16[64,4,128]{2,1,0:T(4,128)(2,1)}), bf16[64,4,128]{2,1,0:T(4,128)(2,1)S(1)}, u32[]{:S(2)}, u32[]{:S(2)}) async-start(bf16[64,4,128]{2,1,0:T(4,128)(2,1)} %broadcast_select_fusion.2), calls=%async_computation | async-start | bytes 131072 | tf_op jit(solution)/shard_map/while/body/eval_jaxpr/all_to_all | solution.py:65
  71.2 6.3 %collective-permute-start = (bf16[128,1]{1,0:T(8,128)(2,1)S(1)}, bf16[128,1]{1,0:T(8,128)(2,1)S(1)}, u32[]{:S(2)}, u32[]{:S(2)}) collective-permute-start(bf16[128,1]{1,0:T(8,128)(2,1)S(1)} %get-tuple-element.170), channel_id=1, source_target_pairs={{1,0},{2,1},{3,2},{5,4},{6,5},{7,6},{9,8},{10,9},{11,10},{13,12},{... | collective-permute-start | bytes 776 | tf_op jit(solution)/shard_map/while/body/eval_jaxpr/ppermute | solution.py:19
  72.5 6.4 %collective-permute-start.1 = (bf16[128,1]{1,0:T(8,128)(2,1)S(1)}, bf16[128,1]{1,0:T(8,128)(2,1)S(1)}, u32[]{:S(2)}, u32[]{:S(2)}) collective-permute-start(bf16[128,1]{1,0:T(8,128)(2,1)S(1)} %get-tuple-element.171), channel_id=1, source_target_pairs={{0,1},{1,2},{2,3},{4,5},{5,6},{6,7},{8,9},{9,10},{10,11},{12,13},{... | collective-permute-start | bytes 776 | tf_op jit(solution)/shard_map/while/body/eval_jaxpr/ppermute | solution.py:16
  81.9 14.4 %all-to-all-start = ((bf16[64,4,128]{2,1,0:T(4,128)(2,1)}), bf16[64,4,128]{2,1,0:T(4,128)(2,1)S(1)}, u32[]{:S(2)}, u32[]{:S(2)}) async-start(bf16[64,4,128]{2,1,0:T(4,128)(2,1)} %broadcast_select_fusion.2), calls=%async_computation | async-start | bytes 131072 | tf_op jit(solution)/shard_map/while/body/eval_jaxpr/all_to_all | solution.py:65
  96.4 6.3 %collective-permute-start = (bf16[128,1]{1,0:T(8,128)(2,1)S(1)}, bf16[128,1]{1,0:T(8,128)(2,1)S(1)}, u32[]{:S(2)}, u32[]{:S(2)}) collective-permute-start(bf16[128,1]{1,0:T(8,128)(2,1)S(1)} %get-tuple-element.170), channel_id=1, source_target_pairs={{1,0},{2,1},{3,2},{5,4},{6,5},{7,6},{9,8},{10,9},{11,10},{13,12},{... | collective-permute-start | bytes 776 | tf_op jit(solution)/shard_map/while/body/eval_jaxpr/ppermute | solution.py:19
  97.7 6.4 %collective-permute-start.1 = (bf16[128,1]{1,0:T(8,128)(2,1)S(1)}, bf16[128,1]{1,0:T(8,128)(2,1)S(1)}, u32[]{:S(2)}, u32[]{:S(2)}) collective-permute-start(bf16[128,1]{1,0:T(8,128)(2,1)S(1)} %get-tuple-element.171), channel_id=1, source_target_pairs={{0,1},{1,2},{2,3},{4,5},{5,6},{6,7},{8,9},{9,10},{10,11},{12,13},{... | collective-permute-start | bytes 776 | tf_op jit(solution)/shard_map/while/body/eval_jaxpr/ppermute | solution.py:16
  107.2 14.4 %all-to-all-start = ((bf16[64,4,128]{2,1,0:T(4,128)(2,1)}), bf16[64,4,128]{2,1,0:T(4,128)(2,1)S(1)}, u32[]{:S(2)}, u32[]{:S(2)}) async-start(bf16[64,4,128]{2,1,0:T(4,128)(2,1)} %broadcast_select_fusion.2), calls=%async_computation | async-start | bytes 131072 | tf_op jit(solution)/shard_map/while/body/eval_jaxpr/all_to_all | solution.py:65
  121.7 6.3 %collective-permute-start = (bf16[128,1]{1,0:T(8,128)(2,1)S(1)}, bf16[128,1]{1,0:T(8,128)(2,1)S(1)}, u32[]{:S(2)}, u32[]{:S(2)}) collective-permute-start(bf16[128,1]{1,0:T(8,128)(2,1)S(1)} %get-tuple-element.170), channel_id=1, source_target_pairs={{1,0},{2,1},{3,2},{5,4},{6,5},{7,6},{9,8},{10,9},{11,10},{13,12},{... | collective-permute-start | bytes 776 | tf_op jit(solution)/shard_map/while/body/eval_jaxpr/ppermute | solution.py:19
  123.0 6.4 %collective-permute-start.1 = (bf16[128,1]{1,0:T(8,128)(2,1)S(1)}, bf16[128,1]{1,0:T(8,128)(2,1)S(1)}, u32[]{:S(2)}, u32[]{:S(2)}) collective-permute-start(bf16[128,1]{1,0:T(8,128)(2,1)S(1)} %get-tuple-element.171), channel_id=1, source_target_pairs={{0,1},{1,2},{2,3},{4,5},{5,6},{6,7},{8,9},{9,10},{10,11},{12,13},{... | collective-permute-start | bytes 776 | tf_op jit(solution)/shard_map/while/body/eval_jaxpr/ppermute | solution.py:16
  132.4 14.4 %all-to-all-start = ((bf16[64,4,128]{2,1,0:T(4,128)(2,1)}), bf16[64,4,128]{2,1,0:T(4,128)(2,1)S(1)}, u32[]{:S(2)}, u32[]{:S(2)}) async-start(bf16[64,4,128]{2,1,0:T(4,128)(2,1)} %broadcast_select_fusion.2), calls=%async_computation | async-start | bytes 131072 | tf_op jit(solution)/shard_map/while/body/eval_jaxpr/all_to_all | solution.py:65
  146.9 6.3 %collective-permute-start = (bf16[128,1]{1,0:T(8,128)(2,1)S(1)}, bf16[128,1]{1,0:T(8,128)(2,1)S(1)}, u32[]{:S(2)}, u32[]{:S(2)}) collective-permute-start(bf16[128,1]{1,0:T(8,128)(2,1)S(1)} %get-tuple-element.170), channel_id=1, source_target_pairs={{1,0},{2,1},{3,2},{5,4},{6,5},{7,6},{9,8},{10,9},{11,10},{13,12},{... | collective-permute-start | bytes 776 | tf_op jit(solution)/shard_map/while/body/eval_jaxpr/ppermute | solution.py:19
  148.2 6.4 %collective-permute-start.1 = (bf16[128,1]{1,0:T(8,128)(2,1)S(1)}, bf16[128,1]{1,0:T(8,128)(2,1)S(1)}, u32[]{:S(2)}, u32[]{:S(2)}) collective-permute-start(bf16[128,1]{1,0:T(8,128)(2,1)S(1)} %get-tuple-element.171), channel_id=1, source_target_pairs={{0,1},{1,2},{2,3},{4,5},{5,6},{6,7},{8,9},{9,10},{10,11},{12,13},{... | collective-permute-start | bytes 776 | tf_op jit(solution)/shard_map/while/body/eval_jaxpr/ppermute | solution.py:16
  157.7 14.4 %all-to-all-start = ((bf16[64,4,128]{2,1,0:T(4,128)(2,1)}), bf16[64,4,128]{2,1,0:T(4,128)(2,1)S(1)}, u32[]{:S(2)}, u32[]{:S(2)}) async-start(bf16[64,4,128]{2,1,0:T(4,128)(2,1)} %broadcast_select_fusion.2), calls=%async_computation | async-start | bytes 131072 | tf_op jit(solution)/shard_map/while/body/eval_jaxpr/all_to_all | solution.py:65
  172.2 6.3 %collective-permute-start = (bf16[128,1]{1,0:T(8,128)(2,1)S(1)}, bf16[128,1]{1,0:T(8,128)(2,1)S(1)}, u32[]{:S(2)}, u32[]{:S(2)}) collective-permute-start(bf16[128,1]{1,0:T(8,128)(2,1)S(1)} %get-tuple-element.170), channel_id=1, source_target_pairs={{1,0},{2,1},{3,2},{5,4},{6,5},{7,6},{9,8},{10,9},{11,10},{13,12},{... | collective-permute-start | bytes 776 | tf_op jit(solution)/shard_map/while/body/eval_jaxpr/ppermute | solution.py:19
  173.5 6.4 %collective-permute-start.1 = (bf16[128,1]{1,0:T(8,128)(2,1)S(1)}, bf16[128,1]{1,0:T(8,128)(2,1)S(1)}, u32[]{:S(2)}, u32[]{:S(2)}) collective-permute-start(bf16[128,1]{1,0:T(8,128)(2,1)S(1)} %get-tuple-element.171), channel_id=1, source_target_pairs={{0,1},{1,2},{2,3},{4,5},{5,6},{6,7},{8,9},{9,10},{10,11},{12,13},{... | collective-permute-start | bytes 776 | tf_op jit(solution)/shard_map/while/body/eval_jaxpr/ppermute | solution.py:16
  182.9 14.4 %all-to-all-start = ((bf16[64,4,128]{2,1,0:T(4,128)(2,1)}), bf16[64,4,128]{2,1,0:T(4,128)(2,1)S(1)}, u32[]{:S(2)}, u32[]{:S(2)}) async-start(bf16[64,4,128]{2,1,0:T(4,128)(2,1)} %broadcast_select_fusion.2), calls=%async_computation | async-start | bytes 131072 | tf_op jit(solution)/shard_map/while/body/eval_jaxpr/all_to_all | solution.py:65
  197.5 6.3 %collective-permute-start = (bf16[128,1]{1,0:T(8,128)(2,1)S(1)}, bf16[128,1]{1,0:T(8,128)(2,1)S(1)}, u32[]{:S(2)}, u32[]{:S(2)}) collective-permute-start(bf16[128,1]{1,0:T(8,128)(2,1)S(1)} %get-tuple-element.170), channel_id=1, source_target_pairs={{1,0},{2,1},{3,2},{5,4},{6,5},{7,6},{9,8},{10,9},{11,10},{13,12},{... | collective-permute-start | bytes 776 | tf_op jit(solution)/shard_map/while/body/eval_jaxpr/ppermute | solution.py:19
  198.7 6.4 %collective-permute-start.1 = (bf16[128,1]{1,0:T(8,128)(2,1)S(1)}, bf16[128,1]{1,0:T(8,128)(2,1)S(1)}, u32[]{:S(2)}, u32[]{:S(2)}) collective-permute-start(bf16[128,1]{1,0:T(8,128)(2,1)S(1)} %get-tuple-element.171), channel_id=1, source_target_pairs={{0,1},{1,2},{2,3},{4,5},{5,6},{6,7},{8,9},{9,10},{10,11},{12,13},{... | collective-permute-start | bytes 776 | tf_op jit(solution)/shard_map/while/body/eval_jaxpr/ppermute | solution.py:16
  208.2 14.4 %all-to-all-start = ((bf16[64,4,128]{2,1,0:T(4,128)(2,1)}), bf16[64,4,128]{2,1,0:T(4,128)(2,1)S(1)}, u32[]{:S(2)}, u32[]{:S(2)}) async-start(bf16[64,4,128]{2,1,0:T(4,128)(2,1)} %broadcast_select_fusion.2), calls=%async_computation | async-start | bytes 131072 | tf_op jit(solution)/shard_map/while/body/eval_jaxpr/all_to_all | solution.py:65
  222.6 248.6 %copy-start = (f32[128,128]{1,0:T(8,128)}, f32[128,128]{1,0:T(8,128)S(1)}, u32[]{:S(2)}) copy-start(f32[128,128]{1,0:T(8,128)S(1)} %get-tuple-element.81) | copy-start | bytes 196612
  222.6 6.0 %copy-start.1 = (s32[1,128,2]{1,2,0:T(2,128)S(1)}, s32[1,128,2]{1,2,0:T(2,128)}, u32[]{:S(2)}) copy-start(s32[1,128,2]{1,2,0:T(2,128)} %param.18) | copy-start | bytes 3076
Sparse Core Ops, SparseCore 0:
  230.2 239.5 all-reduce.2
where the time goes:
time: 480 us; the launch traced here: 478 us
  waiting for transfers between devices  322 us (67%)
  starting transfers between devices  99.5 us (21%)
  matrix products  15.6 us (3%)
  local copies, waits for them, and re-layouts  14.6 us (3%)
  between operations  14.1 us (3%)
  other arithmetic  11.6 us (2%)
    psum x1, waiting for transfers between devices, on_device(): summed = lax.psum(partial_sum, ('tile', 'sec'))  240 us
    all_to_all x8, waiting for transfers between devices, advance_send(): lax.all_to_all(outgoing, 'tile', split_axis=0, concat_axis=0, tiled=True)  70.7 us
    all_to_all x8, starting transfers between devices, advance_send(): lax.all_to_all(outgoing, 'tile', split_axis=0, concat_axis=0, tiled=True)  50.7 us
    ppermute x8, starting transfers between devices, padded_2(): lax.ppermute(lax.slice_in_dim(block, block.shape[dim] - width, None, axis...  38.5 us
    ppermute x8, waiting for transfers between devices, padded_2(): lax.ppermute(lax.slice_in_dim(block, block.shape[dim] - width, None, axis...  11.2 us
    ppermute x8, starting transfers between devices, padded_2(): lax.ppermute(lax.slice_in_dim(block, 0, width, axis=dim), axis, backward)  10.3 us
    dot_general x8, matrix products, cable_update(): jnp.einsum('ci,ji->cj', right_side, inv_cable, precision=lax.Precision.HI...  10.2 us
  transfers between devices with their start and end apart: 25, of which 17 were waited for; matrix products, arithmetic and copies ran while one was open for 0% of the time, Pallas kernels for 0%

commit v1 on v0

--- a/solution.py
+++ b/solution.py
@@ -85,7 +85,8 @@
     )
     partial_sum = jnp.einsum("tskc,skq->tqc", tile_sums, select, precision=lax.Precision.HIGHEST)
     partial_sum = partial_sum.reshape(step_count, tile_total * contact_width)
-    summed = lax.psum(partial_sum, ("tile", "sec"))
+    _keep_up_row = lambda shard_in: lax.psum(lax.psum(shard_in, axis_name="sec"), axis_name="tile")
+    summed = _keep_up_row(partial_sum)
     share_width = summed.shape[1] // (tile_count * section_count)
     position = lax.axis_index("tile") * section_count + lax.axis_index("sec")
     probe_share = lax.dynamic_slice_in_dim(summed, position * share_width, share_width, 1)

time: 480 us -> 463 us (0.965)
  waiting for transfers between devices: 322 us -> 302 us
    psum x1 -> x2, waiting for transfers between devices: 240 us -> 220 us  [the longest x1 176 us: on_device(): lax.psum(lax.psum(shard_in, axis_name='sec'), axis_name='tile')]
  transfers between devices with their start and end apart: 25 -> 26, of which waited for: 17 -> 18; matrix products, arithmetic and copies ran while one was open for 0% -> 0% of each run, Pallas kernels for 0% -> 0%
where the time goes in v1:
time: 463 us; the launch traced here: 459 us
  waiting for transfers between devices  302 us (65%)
  starting transfers between devices  99.5 us (21%)
  matrix products  15.6 us (3%)
  local copies, waits for them, and re-layouts  14.6 us (3%)
  between operations  14.1 us (3%)
  other arithmetic  11.6 us (3%)
    psum x1, waiting for transfers between devices, on_device(): lax.psum(lax.psum(shard_in, axis_name='sec'), axis_name='tile')  176 us
    all_to_all x8, waiting for transfers between devices, advance_send(): lax.all_to_all(outgoing, 'tile', split_axis=0, concat_axis=0, tiled=True)  70.7 us
    all_to_all x8, starting transfers between devices, advance_send(): lax.all_to_all(outgoing, 'tile', split_axis=0, concat_axis=0, tiled=True)  50.6 us
    psum x1, waiting for transfers between devices, on_device(): lax.psum(shard_in, axis_name='sec')  44 us
    ppermute x8, starting transfers between devices, padded_2(): lax.ppermute(lax.slice_in_dim(block, block.shape[dim] - width, None, axis...  38.5 us
    ppermute x8, waiting for transfers between devices, padded_2(): lax.ppermute(lax.slice_in_dim(block, block.shape[dim] - width, None, axis...  11.2 us
    ppermute x8, starting transfers between devices, padded_2(): lax.ppermute(lax.slice_in_dim(block, 0, width, axis=dim), axis, backward)  10.3 us
    dot_general x8, matrix products, cable_update(): jnp.einsum('ci,ji->cj', right_side, inv_cable, precision=lax.Precision.HI...  10.2 us
  transfers between devices with their start and end apart: 26, of which 18 were waited for; matrix products, arithmetic and copies ran while one was open for 0% of the time, Pallas kernels for 0%

profile of v1, /device:TPU:8, one launch (start us, length us, event | category | flops | bytes accessed | tf_op | source)
XLA Modules:
  0.0 458.6 jit_solution(12587647744360017392)
XLA Ops:
  7.2 0.8 copy.38
  12.4 0.9 mul.74
  13.3 1.0 scatter_custom_fusion
  14.3 208.3 %while.13 = (s32[]{:T(128)}, f32[128,128]{1,0:T(8,128)S(1)}, bf16[8,64,4,128]{3,2,1,0:T(4,128)(2,1)S(1)}, f32[128,128]{1,0:T(8,128)}, bf16[8,128,128]{2,1,0:T(8,...) while((s32[]{:T(128)}, f32[128,128]{1,0:T(8,128)S(1)}, ...), condition=%wide.region_4.5_spmd, body=%wide.region_3.4_spmd.sunk | while | flops 25629952 | bytes 1626603 | solution.py:68
  14.4 1.3 collective-permute-start
  15.7 4.5 collective-permute-start.1
  20.4 1.4 collective-permute-done.1
  21.9 1.3 fusion.52
  23.2 0.9 gather_fusion
  24.8 12.1 %all-to-all-start = ((bf16[64,4,128]{2,1,0:T(4,128)(2,1)}), bf16[64,4,128]{2,1,0:T(4,128)(2,1)S(1)}, u32[]{:S(2)}, u32[]{:S(2)}) async-start(bf16[64,4,128]{2,1,0:T(4,128)(2,1)} %broadcast_select_fusion.2), calls=%async_computation | async-start | bytes 131072 | tf_op jit(solution)/shard_map/while/body/eval_jaxpr/all_to_all | solution.py:65
  36.9 8.8 %all-to-all-done = bf16[64,4,128]{2,1,0:T(4,128)(2,1)S(1)} async-done(((bf16[64,4,128]{2,1,0:T(4,128)(2,1)}), bf16[64,4,128]{2,1,0:T(4,128)(2,1)S(1)}, u32[]{:S(2)}, u32[]{:S(2)}) %all-to-all-start) | async-done | bytes 65568 | tf_op jit(solution)/shard_map/while/body/eval_jaxpr/all_to_all | solution.py:65
  45.9 1.3 collective-permute-start
  47.2 4.9 %collective-permute-start.1 = (bf16[128,1]{1,0:T(8,128)(2,1)S(1)}, bf16[128,1]{1,0:T(8,128)(2,1)S(1)}, u32[]{:S(2)}, u32[]{:S(2)}) collective-permute-start(bf16[128,1]{1,0:T(8,128)(2,1)S(1)} %get-tuple-element.171), channel_id=1, source_target_pairs={{0,1},{1,2},{2,3},{4,5},{5,6},{6,7},{8,9},{9,10},{10,11},{12,13},{... | collective-permute-start | bytes 776 | tf_op jit(solution)/shard_map/while/body/eval_jaxpr/ppermute | solution.py:16
  52.2 1.4 collective-permute-done.1
  53.7 1.3 fusion.52
  55.0 0.9 gather_fusion
  56.7 5.5 %all-to-all-start = ((bf16[64,4,128]{2,1,0:T(4,128)(2,1)}), bf16[64,4,128]{2,1,0:T(4,128)(2,1)S(1)}, u32[]{:S(2)}, u32[]{:S(2)}) async-start(bf16[64,4,128]{2,1,0:T(4,128)(2,1)} %broadcast_select_fusion.2), calls=%async_computation | async-start | bytes 131072 | tf_op jit(solution)/shard_map/while/body/eval_jaxpr/all_to_all | solution.py:65
  62.2 8.8 %all-to-all-done = bf16[64,4,128]{2,1,0:T(4,128)(2,1)S(1)} async-done(((bf16[64,4,128]{2,1,0:T(4,128)(2,1)}), bf16[64,4,128]{2,1,0:T(4,128)(2,1)S(1)}, u32[]{:S(2)}, u32[]{:S(2)}) %all-to-all-start) | async-done | bytes 65568 | tf_op jit(solution)/shard_map/while/body/eval_jaxpr/all_to_all | solution.py:65
  71.2 1.3 collective-permute-start
  72.5 4.9 %collective-permute-start.1 = (bf16[128,1]{1,0:T(8,128)(2,1)S(1)}, bf16[128,1]{1,0:T(8,128)(2,1)S(1)}, u32[]{:S(2)}, u32[]{:S(2)}) collective-permute-start(bf16[128,1]{1,0:T(8,128)(2,1)S(1)} %get-tuple-element.171), channel_id=1, source_target_pairs={{0,1},{1,2},{2,3},{4,5},{5,6},{6,7},{8,9},{9,10},{10,11},{12,13},{... | collective-permute-start | bytes 776 | tf_op jit(solution)/shard_map/while/body/eval_jaxpr/ppermute | solution.py:16
  77.5 1.4 collective-permute-done.1
  79.0 1.3 fusion.52
  80.3 0.9 gather_fusion
  81.9 5.5 %all-to-all-start = ((bf16[64,4,128]{2,1,0:T(4,128)(2,1)}), bf16[64,4,128]{2,1,0:T(4,128)(2,1)S(1)}, u32[]{:S(2)}, u32[]{:S(2)}) async-start(bf16[64,4,128]{2,1,0:T(4,128)(2,1)} %broadcast_select_fusion.2), calls=%async_computation | async-start | bytes 131072 | tf_op jit(solution)/shard_map/while/body/eval_jaxpr/all_to_all | solution.py:65
  87.4 8.8 %all-to-all-done = bf16[64,4,128]{2,1,0:T(4,128)(2,1)S(1)} async-done(((bf16[64,4,128]{2,1,0:T(4,128)(2,1)}), bf16[64,4,128]{2,1,0:T(4,128)(2,1)S(1)}, u32[]{:S(2)}, u32[]{:S(2)}) %all-to-all-start) | async-done | bytes 65568 | tf_op jit(solution)/shard_map/while/body/eval_jaxpr/all_to_all | solution.py:65
  96.4 1.3 collective-permute-start
  97.7 4.9 %collective-permute-start.1 = (bf16[128,1]{1,0:T(8,128)(2,1)S(1)}, bf16[128,1]{1,0:T(8,128)(2,1)S(1)}, u32[]{:S(2)}, u32[]{:S(2)}) collective-permute-start(bf16[128,1]{1,0:T(8,128)(2,1)S(1)} %get-tuple-element.171), channel_id=1, source_target_pairs={{0,1},{1,2},{2,3},{4,5},{5,6},{6,7},{8,9},{9,10},{10,11},{12,13},{... | collective-permute-start | bytes 776 | tf_op jit(solution)/shard_map/while/body/eval_jaxpr/ppermute | solution.py:16
  102.8 1.4 collective-permute-done.1
  104.3 1.3 fusion.52
  105.5 0.9 gather_fusion
  107.2 5.5 %all-to-all-start = ((bf16[64,4,128]{2,1,0:T(4,128)(2,1)}), bf16[64,4,128]{2,1,0:T(4,128)(2,1)S(1)}, u32[]{:S(2)}, u32[]{:S(2)}) async-start(bf16[64,4,128]{2,1,0:T(4,128)(2,1)} %broadcast_select_fusion.2), calls=%async_computation | async-start | bytes 131072 | tf_op jit(solution)/shard_map/while/body/eval_jaxpr/all_to_all | solution.py:65
  112.7 8.8 %all-to-all-done = bf16[64,4,128]{2,1,0:T(4,128)(2,1)S(1)} async-done(((bf16[64,4,128]{2,1,0:T(4,128)(2,1)}), bf16[64,4,128]{2,1,0:T(4,128)(2,1)S(1)}, u32[]{:S(2)}, u32[]{:S(2)}) %all-to-all-start) | async-done | bytes 65568 | tf_op jit(solution)/shard_map/while/body/eval_jaxpr/all_to_all | solution.py:65
  121.7 1.3 collective-permute-start
  123.0 4.8 %collective-permute-start.1 = (bf16[128,1]{1,0:T(8,128)(2,1)S(1)}, bf16[128,1]{1,0:T(8,128)(2,1)S(1)}, u32[]{:S(2)}, u32[]{:S(2)}) collective-permute-start(bf16[128,1]{1,0:T(8,128)(2,1)S(1)} %get-tuple-element.171), channel_id=1, source_target_pairs={{0,1},{1,2},{2,3},{4,5},{5,6},{6,7},{8,9},{9,10},{10,11},{12,13},{... | collective-permute-start | bytes 776 | tf_op jit(solution)/shard_map/while/body/eval_jaxpr/ppermute | solution.py:16
  128.0 1.4 collective-permute-done.1
  129.5 1.3 fusion.52
  130.8 0.9 gather_fusion
  132.4 5.5 %all-to-all-start = ((bf16[64,4,128]{2,1,0:T(4,128)(2,1)}), bf16[64,4,128]{2,1,0:T(4,128)(2,1)S(1)}, u32[]{:S(2)}, u32[]{:S(2)}) async-start(bf16[64,4,128]{2,1,0:T(4,128)(2,1)} %broadcast_select_fusion.2), calls=%async_computation | async-start | bytes 131072 | tf_op jit(solution)/shard_map/while/body/eval_jaxpr/all_to_all | solution.py:65
  137.9 8.8 %all-to-all-done = bf16[64,4,128]{2,1,0:T(4,128)(2,1)S(1)} async-done(((bf16[64,4,128]{2,1,0:T(4,128)(2,1)}), bf16[64,4,128]{2,1,0:T(4,128)(2,1)S(1)}, u32[]{:S(2)}, u32[]{:S(2)}) %all-to-all-start) | async-done | bytes 65568 | tf_op jit(solution)/shard_map/while/body/eval_jaxpr/all_to_all | solution.py:65
  146.9 1.3 collective-permute-start
  148.2 4.9 %collective-permute-start.1 = (bf16[128,1]{1,0:T(8,128)(2,1)S(1)}, bf16[128,1]{1,0:T(8,128)(2,1)S(1)}, u32[]{:S(2)}, u32[]{:S(2)}) collective-permute-start(bf16[128,1]{1,0:T(8,128)(2,1)S(1)} %get-tuple-element.171), channel_id=1, source_target_pairs={{0,1},{1,2},{2,3},{4,5},{5,6},{6,7},{8,9},{9,10},{10,11},{12,13},{... | collective-permute-start | bytes 776 | tf_op jit(solution)/shard_map/while/body/eval_jaxpr/ppermute | solution.py:16
  153.3 1.4 collective-permute-done.1
  154.8 1.3 fusion.52
  156.0 0.9 gather_fusion
  157.7 5.5 %all-to-all-start = ((bf16[64,4,128]{2,1,0:T(4,128)(2,1)}), bf16[64,4,128]{2,1,0:T(4,128)(2,1)S(1)}, u32[]{:S(2)}, u32[]{:S(2)}) async-start(bf16[64,4,128]{2,1,0:T(4,128)(2,1)} %broadcast_select_fusion.2), calls=%async_computation | async-start | bytes 131072 | tf_op jit(solution)/shard_map/while/body/eval_jaxpr/all_to_all | solution.py:65
  163.2 8.8 %all-to-all-done = bf16[64,4,128]{2,1,0:T(4,128)(2,1)S(1)} async-done(((bf16[64,4,128]{2,1,0:T(4,128)(2,1)}), bf16[64,4,128]{2,1,0:T(4,128)(2,1)S(1)}, u32[]{:S(2)}, u32[]{:S(2)}) %all-to-all-start) | async-done | bytes 65568 | tf_op jit(solution)/shard_map/while/body/eval_jaxpr/all_to_all | solution.py:65
  172.2 1.3 collective-permute-start
  173.5 4.9 %collective-permute-start.1 = (bf16[128,1]{1,0:T(8,128)(2,1)S(1)}, bf16[128,1]{1,0:T(8,128)(2,1)S(1)}, u32[]{:S(2)}, u32[]{:S(2)}) collective-permute-start(bf16[128,1]{1,0:T(8,128)(2,1)S(1)} %get-tuple-element.171), channel_id=1, source_target_pairs={{0,1},{1,2},{2,3},{4,5},{5,6},{6,7},{8,9},{9,10},{10,11},{12,13},{... | collective-permute-start | bytes 776 | tf_op jit(solution)/shard_map/while/body/eval_jaxpr/ppermute | solution.py:16
  178.5 1.4 collective-permute-done.1
  180.0 1.3 fusion.52
  181.3 0.9 gather_fusion
  182.9 5.5 %all-to-all-start = ((bf16[64,4,128]{2,1,0:T(4,128)(2,1)}), bf16[64,4,128]{2,1,0:T(4,128)(2,1)S(1)}, u32[]{:S(2)}, u32[]{:S(2)}) async-start(bf16[64,4,128]{2,1,0:T(4,128)(2,1)} %broadcast_select_fusion.2), calls=%async_computation | async-start | bytes 131072 | tf_op jit(solution)/shard_map/while/body/eval_jaxpr/all_to_all | solution.py:65
  188.4 8.8 %all-to-all-done = bf16[64,4,128]{2,1,0:T(4,128)(2,1)S(1)} async-done(((bf16[64,4,128]{2,1,0:T(4,128)(2,1)}), bf16[64,4,128]{2,1,0:T(4,128)(2,1)S(1)}, u32[]{:S(2)}, u32[]{:S(2)}) %all-to-all-start) | async-done | bytes 65568 | tf_op jit(solution)/shard_map/while/body/eval_jaxpr/all_to_all | solution.py:65
  197.4 1.3 collective-permute-start
  198.7 4.8 %collective-permute-start.1 = (bf16[128,1]{1,0:T(8,128)(2,1)S(1)}, bf16[128,1]{1,0:T(8,128)(2,1)S(1)}, u32[]{:S(2)}, u32[]{:S(2)}) collective-permute-start(bf16[128,1]{1,0:T(8,128)(2,1)S(1)} %get-tuple-element.171), channel_id=1, source_target_pairs={{0,1},{1,2},{2,3},{4,5},{5,6},{6,7},{8,9},{9,10},{10,11},{12,13},{... | collective-permute-start | bytes 776 | tf_op jit(solution)/shard_map/while/body/eval_jaxpr/ppermute | solution.py:16
  203.8 1.4 collective-permute-done.1
  205.3 1.3 fusion.52
  206.5 0.9 gather_fusion
  208.2 5.5 %all-to-all-start = ((bf16[64,4,128]{2,1,0:T(4,128)(2,1)}), bf16[64,4,128]{2,1,0:T(4,128)(2,1)S(1)}, u32[]{:S(2)}, u32[]{:S(2)}) async-start(bf16[64,4,128]{2,1,0:T(4,128)(2,1)} %broadcast_select_fusion.2), calls=%async_computation | async-start | bytes 131072 | tf_op jit(solution)/shard_map/while/body/eval_jaxpr/all_to_all | solution.py:65
  213.7 8.8 %all-to-all-done = bf16[64,4,128]{2,1,0:T(4,128)(2,1)S(1)} async-done(((bf16[64,4,128]{2,1,0:T(4,128)(2,1)}), bf16[64,4,128]{2,1,0:T(4,128)(2,1)S(1)}, u32[]{:S(2)}, u32[]{:S(2)}) %all-to-all-start) | async-done | bytes 65568 | tf_op jit(solution)/shard_map/while/body/eval_jaxpr/all_to_all | solution.py:65
  223.9 4.6 %fusion.28 = f32[8,128,2,128]{3,0,2,1:T(8,128)S(1)} fusion(bf16[1,128,2,128,128]{4,3,2,1,0:T(8,128)(2,1)} %param.19, bf16[128,8,128]{2,1,0:T(8,128)(2,1)S(1)} %gather_fusion.1, pred[128]{0:T(512)(128)(4,1)S(1)} %compare_and_fusion.1), kind=kOutput, calls=%fused_computation.41 | convolution fusion | flops 67239936 | bytes 9699456 | tf_op jit(solution)/shard_map/tsi,skic->tskc/dot_general | solution.py:82
  230.1 44.0 %all-reduce.4.cloned.1.call-done = f32[8,4096]{1,0:T(8,128)} async-done(((f32[8,4096]{1,0:T(8,128)}), f32[8,4096]{1,0:T(8,128)}) %all-reduce.4.cloned.1.call-update) | async-done | bytes 131088 | tf_op jit(solution)/shard_map/psum | solution.py:88
  274.2 176.3 %all-reduce.6.cloned.1.call-done = f32[8,4096]{1,0:T(8,128)} async-done(((f32[8,4096]{1,0:T(8,128)}), f32[8,4096]{1,0:T(8,128)}) %all-reduce.6.cloned.1.call-update) | async-done | bytes 131088 | tf_op jit(solution)/shard_map/psum | solution.py:88
  450.5 1.3 constant_dynamic-slice_fusion
  (131 shorter events, 16.3 us)
Async XLA Ops:
  7.2 267.0 %all-reduce.4.cloned.1.call-start = ((), (), s32[]{:S(2)}) async-start(), calls=%async_computation.1 | async-start | bytes 262144 | tf_op jit(solution)/shard_map/psum | solution.py:88
  14.4 6.0 %collective-permute-start = (bf16[128,1]{1,0:T(8,128)(2,1)S(1)}, bf16[128,1]{1,0:T(8,128)(2,1)S(1)}, u32[]{:S(2)}, u32[]{:S(2)}) collective-permute-start(bf16[128,1]{1,0:T(8,128)(2,1)S(1)} %get-tuple-element.170), channel_id=1, source_target_pairs={{1,0},{2,1},{3,2},{5,4},{6,5},{7,6},{9,8},{10,9},{11,10},{13,12},{... | collective-permute-start | bytes 776 | tf_op jit(solution)/shard_map/while/body/eval_jaxpr/ppermute | solution.py:19
  15.7 6.1 %collective-permute-start.1 = (bf16[128,1]{1,0:T(8,128)(2,1)S(1)}, bf16[128,1]{1,0:T(8,128)(2,1)S(1)}, u32[]{:S(2)}, u32[]{:S(2)}) collective-permute-start(bf16[128,1]{1,0:T(8,128)(2,1)S(1)} %get-tuple-element.171), channel_id=1, source_target_pairs={{0,1},{1,2},{2,3},{4,5},{5,6},{6,7},{8,9},{9,10},{10,11},{12,13},{... | collective-permute-start | bytes 776 | tf_op jit(solution)/shard_map/while/body/eval_jaxpr/ppermute | solution.py:16
  24.8 20.9 %all-to-all-start = ((bf16[64,4,128]{2,1,0:T(4,128)(2,1)}), bf16[64,4,128]{2,1,0:T(4,128)(2,1)S(1)}, u32[]{:S(2)}, u32[]{:S(2)}) async-start(bf16[64,4,128]{2,1,0:T(4,128)(2,1)} %broadcast_select_fusion.2), calls=%async_computation | async-start | bytes 131072 | tf_op jit(solution)/shard_map/while/body/eval_jaxpr/all_to_all | solution.py:65
  45.9 6.3 %collective-permute-start = (bf16[128,1]{1,0:T(8,128)(2,1)S(1)}, bf16[128,1]{1,0:T(8,128)(2,1)S(1)}, u32[]{:S(2)}, u32[]{:S(2)}) collective-permute-start(bf16[128,1]{1,0:T(8,128)(2,1)S(1)} %get-tuple-element.170), channel_id=1, source_target_pairs={{1,0},{2,1},{3,2},{5,4},{6,5},{7,6},{9,8},{10,9},{11,10},{13,12},{... | collective-permute-start | bytes 776 | tf_op jit(solution)/shard_map/while/body/eval_jaxpr/ppermute | solution.py:19
  47.2 6.4 %collective-permute-start.1 = (bf16[128,1]{1,0:T(8,128)(2,1)S(1)}, bf16[128,1]{1,0:T(8,128)(2,1)S(1)}, u32[]{:S(2)}, u32[]{:S(2)}) collective-permute-start(bf16[128,1]{1,0:T(8,128)(2,1)S(1)} %get-tuple-element.171), channel_id=1, source_target_pairs={{0,1},{1,2},{2,3},{4,5},{5,6},{6,7},{8,9},{9,10},{10,11},{12,13},{... | collective-permute-start | bytes 776 | tf_op jit(solution)/shard_map/while/body/eval_jaxpr/ppermute | solution.py:16
  56.7 14.4 %all-to-all-start = ((bf16[64,4,128]{2,1,0:T(4,128)(2,1)}), bf16[64,4,128]{2,1,0:T(4,128)(2,1)S(1)}, u32[]{:S(2)}, u32[]{:S(2)}) async-start(bf16[64,4,128]{2,1,0:T(4,128)(2,1)} %broadcast_select_fusion.2), calls=%async_computation | async-start | bytes 131072 | tf_op jit(solution)/shard_map/while/body/eval_jaxpr/all_to_all | solution.py:65
  71.2 6.3 %collective-permute-start = (bf16[128,1]{1,0:T(8,128)(2,1)S(1)}, bf16[128,1]{1,0:T(8,128)(2,1)S(1)}, u32[]{:S(2)}, u32[]{:S(2)}) collective-permute-start(bf16[128,1]{1,0:T(8,128)(2,1)S(1)} %get-tuple-element.170), channel_id=1, source_target_pairs={{1,0},{2,1},{3,2},{5,4},{6,5},{7,6},{9,8},{10,9},{11,10},{13,12},{... | collective-permute-start | bytes 776 | tf_op jit(solution)/shard_map/while/body/eval_jaxpr/ppermute | solution.py:19
  72.5 6.4 %collective-permute-start.1 = (bf16[128,1]{1,0:T(8,128)(2,1)S(1)}, bf16[128,1]{1,0:T(8,128)(2,1)S(1)}, u32[]{:S(2)}, u32[]{:S(2)}) collective-permute-start(bf16[128,1]{1,0:T(8,128)(2,1)S(1)} %get-tuple-element.171), channel_id=1, source_target_pairs={{0,1},{1,2},{2,3},{4,5},{5,6},{6,7},{8,9},{9,10},{10,11},{12,13},{... | collective-permute-start | bytes 776 | tf_op jit(solution)/shard_map/while/body/eval_jaxpr/ppermute | solution.py:16
  81.9 14.3 %all-to-all-start = ((bf16[64,4,128]{2,1,0:T(4,128)(2,1)}), bf16[64,4,128]{2,1,0:T(4,128)(2,1)S(1)}, u32[]{:S(2)}, u32[]{:S(2)}) async-start(bf16[64,4,128]{2,1,0:T(4,128)(2,1)} %broadcast_select_fusion.2), calls=%async_computation | async-start | bytes 131072 | tf_op jit(solution)/shard_map/while/body/eval_jaxpr/all_to_all | solution.py:65
  96.4 6.3 %collective-permute-start = (bf16[128,1]{1,0:T(8,128)(2,1)S(1)}, bf16[128,1]{1,0:T(8,128)(2,1)S(1)}, u32[]{:S(2)}, u32[]{:S(2)}) collective-permute-start(bf16[128,1]{1,0:T(8,128)(2,1)S(1)} %get-tuple-element.170), channel_id=1, source_target_pairs={{1,0},{2,1},{3,2},{5,4},{6,5},{7,6},{9,8},{10,9},{11,10},{13,12},{... | collective-permute-start | bytes 776 | tf_op jit(solution)/shard_map/while/body/eval_jaxpr/ppermute | solution.py:19
  97.7 6.4 %collective-permute-start.1 = (bf16[128,1]{1,0:T(8,128)(2,1)S(1)}, bf16[128,1]{1,0:T(8,128)(2,1)S(1)}, u32[]{:S(2)}, u32[]{:S(2)}) collective-permute-start(bf16[128,1]{1,0:T(8,128)(2,1)S(1)} %get-tuple-element.171), channel_id=1, source_target_pairs={{0,1},{1,2},{2,3},{4,5},{5,6},{6,7},{8,9},{9,10},{10,11},{12,13},{... | collective-permute-start | bytes 776 | tf_op jit(solution)/shard_map/while/body/eval_jaxpr/ppermute | solution.py:16
  107.2 14.3 %all-to-all-start = ((bf16[64,4,128]{2,1,0:T(4,128)(2,1)}), bf16[64,4,128]{2,1,0:T(4,128)(2,1)S(1)}, u32[]{:S(2)}, u32[]{:S(2)}) async-start(bf16[64,4,128]{2,1,0:T(4,128)(2,1)} %broadcast_select_fusion.2), calls=%async_computation | async-start | bytes 131072 | tf_op jit(solution)/shard_map/while/body/eval_jaxpr/all_to_all | solution.py:65
  121.7 6.3 %collective-permute-start = (bf16[128,1]{1,0:T(8,128)(2,1)S(1)}, bf16[128,1]{1,0:T(8,128)(2,1)S(1)}, u32[]{:S(2)}, u32[]{:S(2)}) collective-permute-start(bf16[128,1]{1,0:T(8,128)(2,1)S(1)} %get-tuple-element.170), channel_id=1, source_target_pairs={{1,0},{2,1},{3,2},{5,4},{6,5},{7,6},{9,8},{10,9},{11,10},{13,12},{... | collective-permute-start | bytes 776 | tf_op jit(solution)/shard_map/while/body/eval_jaxpr/ppermute | solution.py:19
  123.0 6.4 %collective-permute-start.1 = (bf16[128,1]{1,0:T(8,128)(2,1)S(1)}, bf16[128,1]{1,0:T(8,128)(2,1)S(1)}, u32[]{:S(2)}, u32[]{:S(2)}) collective-permute-start(bf16[128,1]{1,0:T(8,128)(2,1)S(1)} %get-tuple-element.171), channel_id=1, source_target_pairs={{0,1},{1,2},{2,3},{4,5},{5,6},{6,7},{8,9},{9,10},{10,11},{12,13},{... | collective-permute-start | bytes 776 | tf_op jit(solution)/shard_map/while/body/eval_jaxpr/ppermute | solution.py:16
  132.4 14.4 %all-to-all-start = ((bf16[64,4,128]{2,1,0:T(4,128)(2,1)}), bf16[64,4,128]{2,1,0:T(4,128)(2,1)S(1)}, u32[]{:S(2)}, u32[]{:S(2)}) async-start(bf16[64,4,128]{2,1,0:T(4,128)(2,1)} %broadcast_select_fusion.2), calls=%async_computation | async-start | bytes 131072 | tf_op jit(solution)/shard_map/while/body/eval_jaxpr/all_to_all | solution.py:65
  146.9 6.3 %collective-permute-start = (bf16[128,1]{1,0:T(8,128)(2,1)S(1)}, bf16[128,1]{1,0:T(8,128)(2,1)S(1)}, u32[]{:S(2)}, u32[]{:S(2)}) collective-permute-start(bf16[128,1]{1,0:T(8,128)(2,1)S(1)} %get-tuple-element.170), channel_id=1, source_target_pairs={{1,0},{2,1},{3,2},{5,4},{6,5},{7,6},{9,8},{10,9},{11,10},{13,12},{... | collective-permute-start | bytes 776 | tf_op jit(solution)/shard_map/while/body/eval_jaxpr/ppermute | solution.py:19
  148.2 6.4 %collective-permute-start.1 = (bf16[128,1]{1,0:T(8,128)(2,1)S(1)}, bf16[128,1]{1,0:T(8,128)(2,1)S(1)}, u32[]{:S(2)}, u32[]{:S(2)}) collective-permute-start(bf16[128,1]{1,0:T(8,128)(2,1)S(1)} %get-tuple-element.171), channel_id=1, source_target_pairs={{0,1},{1,2},{2,3},{4,5},{5,6},{6,7},{8,9},{9,10},{10,11},{12,13},{... | collective-permute-start | bytes 776 | tf_op jit(solution)/shard_map/while/body/eval_jaxpr/ppermute | solution.py:16
  157.7 14.3 %all-to-all-start = ((bf16[64,4,128]{2,1,0:T(4,128)(2,1)}), bf16[64,4,128]{2,1,0:T(4,128)(2,1)S(1)}, u32[]{:S(2)}, u32[]{:S(2)}) async-start(bf16[64,4,128]{2,1,0:T(4,128)(2,1)} %broadcast_select_fusion.2), calls=%async_computation | async-start | bytes 131072 | tf_op jit(solution)/shard_map/while/body/eval_jaxpr/all_to_all | solution.py:65
  172.2 6.3 %collective-permute-start = (bf16[128,1]{1,0:T(8,128)(2,1)S(1)}, bf16[128,1]{1,0:T(8,128)(2,1)S(1)}, u32[]{:S(2)}, u32[]{:S(2)}) collective-permute-start(bf16[128,1]{1,0:T(8,128)(2,1)S(1)} %get-tuple-element.170), channel_id=1, source_target_pairs={{1,0},{2,1},{3,2},{5,4},{6,5},{7,6},{9,8},{10,9},{11,10},{13,12},{... | collective-permute-start | bytes 776 | tf_op jit(solution)/shard_map/while/body/eval_jaxpr/ppermute | solution.py:19
  173.5 6.4 %collective-permute-start.1 = (bf16[128,1]{1,0:T(8,128)(2,1)S(1)}, bf16[128,1]{1,0:T(8,128)(2,1)S(1)}, u32[]{:S(2)}, u32[]{:S(2)}) collective-permute-start(bf16[128,1]{1,0:T(8,128)(2,1)S(1)} %get-tuple-element.171), channel_id=1, source_target_pairs={{0,1},{1,2},{2,3},{4,5},{5,6},{6,7},{8,9},{9,10},{10,11},{12,13},{... | collective-permute-start | bytes 776 | tf_op jit(solution)/shard_map/while/body/eval_jaxpr/ppermute | solution.py:16
  182.9 14.3 %all-to-all-start = ((bf16[64,4,128]{2,1,0:T(4,128)(2,1)}), bf16[64,4,128]{2,1,0:T(4,128)(2,1)S(1)}, u32[]{:S(2)}, u32[]{:S(2)}) async-start(bf16[64,4,128]{2,1,0:T(4,128)(2,1)} %broadcast_select_fusion.2), calls=%async_computation | async-start | bytes 131072 | tf_op jit(solution)/shard_map/while/body/eval_jaxpr/all_to_all | solution.py:65
  197.4 6.3 %collective-permute-start = (bf16[128,1]{1,0:T(8,128)(2,1)S(1)}, bf16[128,1]{1,0:T(8,128)(2,1)S(1)}, u32[]{:S(2)}, u32[]{:S(2)}) collective-permute-start(bf16[128,1]{1,0:T(8,128)(2,1)S(1)} %get-tuple-element.170), channel_id=1, source_target_pairs={{1,0},{2,1},{3,2},{5,4},{6,5},{7,6},{9,8},{10,9},{11,10},{13,12},{... | collective-permute-start | bytes 776 | tf_op jit(solution)/shard_map/while/body/eval_jaxpr/ppermute | solution.py:19
  198.7 6.4 %collective-permute-start.1 = (bf16[128,1]{1,0:T(8,128)(2,1)S(1)}, bf16[128,1]{1,0:T(8,128)(2,1)S(1)}, u32[]{:S(2)}, u32[]{:S(2)}) collective-permute-start(bf16[128,1]{1,0:T(8,128)(2,1)S(1)} %get-tuple-element.171), channel_id=1, source_target_pairs={{0,1},{1,2},{2,3},{4,5},{5,6},{6,7},{8,9},{9,10},{10,11},{12,13},{... | collective-permute-start | bytes 776 | tf_op jit(solution)/shard_map/while/body/eval_jaxpr/ppermute | solution.py:16
  208.2 14.3 %all-to-all-start = ((bf16[64,4,128]{2,1,0:T(4,128)(2,1)}), bf16[64,4,128]{2,1,0:T(4,128)(2,1)S(1)}, u32[]{:S(2)}, u32[]{:S(2)}) async-start(bf16[64,4,128]{2,1,0:T(4,128)(2,1)} %broadcast_select_fusion.2), calls=%async_computation | async-start | bytes 131072 | tf_op jit(solution)/shard_map/while/body/eval_jaxpr/all_to_all | solution.py:65
  222.6 229.2 %copy-start = (f32[128,128]{1,0:T(8,128)}, f32[128,128]{1,0:T(8,128)S(1)}, u32[]{:S(2)}) copy-start(f32[128,128]{1,0:T(8,128)S(1)} %get-tuple-element.81) | copy-start | bytes 196612
  222.6 6.0 %copy-start.1 = (s32[1,128,2]{1,2,0:T(2,128)S(1)}, s32[1,128,2]{1,2,0:T(2,128)}, u32[]{:S(2)}) copy-start(s32[1,128,2]{1,2,0:T(2,128)} %param.18) | copy-start | bytes 3076
  230.1 220.4 %all-reduce.6.cloned.1.call-start = ((), (), s32[]{:S(2)}) async-start(), calls=%async_computation.2 | async-start | bytes 262144 | tf_op jit(solution)/shard_map/psum | solution.py:88
Sparse Core Ops, SparseCore 0:
  230.2 43.9 all-reduce.3
  278.0 172.4 all-reduce.5
